TPU v7x, 32 devices: a whole 2x2x4 slice. The times are simulated.
32 devices in a mesh: tx: 4 (over x, core), ty: 4 (over z), solver: 2 (over y).
Axes of the slice: x: 2, y: 2, z: 4, core: 2. Of those that a mesh axis runs over, the one named last changes fastest.
Arguments:
- particle_state: float32 [8, 131072], P(None, ('tx', 'ty', 'solver')), as said below
- particle_cell: int32 [131072], P(('tx', 'ty', 'solver')), may hold values from 0 to 8191
- boundary_list: int32 [4, 4, 2, 2, 2, 256], P('tx', 'ty', 'solver'), may hold values from 0 to 4095
- boundary_count: int32 [4, 4, 2, 2, 2], P('tx', 'ty', 'solver'), may hold values from 128 to 256, as said below
- contact_own: int32 [4, 4, 2, 16384], P('tx', 'ty', 'solver'), may hold values from 0 to 4095
- contact_other: int32 [4, 4, 2, 16384], P('tx', 'ty', 'solver'), may hold values from 0 to 14335, as said below
- contact_count: int32 [4, 4, 2], P('tx', 'ty', 'solver'), may hold values from 1 to 16384, as said below
- gas_velocity: float32 [3, 16, 16, 512], P(None, 'solver', 'tx', 'ty'), may hold values from -6 to 6
- gas_source: float32 [3, 16, 16, 512], P(None, 'solver', 'tx', 'ty'), may hold values from -3 to 3
Outputs:
- particle_velocity: float32 [3, 131072], P(None, ('tx', 'ty', 'solver'))
- gas_velocity_new: float32 [3, 16, 16, 512], P(None, 'solver', 'tx', 'ty')
Inputs may be any that keep to these rules, and one draw needn't show every extreme that they name: `boundary_count`: some quadrant list holds all 256 live entries. `contact_other`: never the tile column h * 4096 + contact_own of the same slot. The live slots of a device are its first contact_count; some device fills all 16384. `particle_state`: position rows in 0 to 1, radius in 0.3 to 0.7, mass in 0.5 to 2.
All inputs are finite; a program needn't handle non-finite values.
Results may differ from a plain program's by a relative error of at most 0.0003.
Values sent between devices are 32-bit elements; how exact they have to be, the bound alone decides.
A program may use at most 64 MiB of HBM per device.

v0:
```python
import jax
import jax.numpy as jnp
import numpy as np
from jax import lax
from jax.sharding import PartitionSpec as P

ITERS = 16


FAR = 100.0
STIFF = 4.0
DAMPING = 1.0
FLOOR = 0.1
BETA_RATE = 2.0
VOLUME = 4.18879
TIME_STEP = 0.1
GRAVITY = 1.0
VISCOSITY = 1.0


def extended(block, sides, width):
    for axis, dim in sides:
        count = lax.axis_size(axis)
        forward = [(i, i + 1) for i in range(count - 1)]
        forward.append((count - 1, 0))
        backward = [(target, source) for source, target in forward]
        low = lax.ppermute(
            lax.slice_in_dim(block, block.shape[dim] - width, None, axis=dim), axis, forward
        )
        high = lax.ppermute(lax.slice_in_dim(block, 0, width, axis=dim), axis, backward)
        block = jnp.concatenate([low, block, high], axis=dim)
    return block


def cycle_layout():
    shifts = [-1, 0, 0, 1]
    slot_list = []
    x_shift = []
    y_shift = []
    for row_pos in range(4):
        for col_pos in range(4):
            if row_pos in (1, 2) and col_pos in (1, 2):
                continue
            slot_list.append(row_pos * 4 + col_pos)
            x_shift.append(shifts[row_pos])
            y_shift.append(shifts[col_pos])
    offsets = np.zeros((8, len(slot_list), 1), np.float32)
    offsets[0, :, 0] = x_shift
    offsets[1, :, 0] = y_shift
    return (np.array(slot_list), offsets)


def pick_quadrants(state, lists, counts):
    list_width = lists.shape[-1]
    picked = jnp.take(state, lists.reshape(-1), axis=1).reshape(8, 2, 2, list_width)
    live_mask = jnp.arange(list_width, dtype=jnp.int32)[None, None, :] < counts[:, :, None]
    filler = jnp.array([FAR, FAR, FAR, 0.0, 0.0, 0.0, 0.0, 0.0], state.dtype)[:, None, None, None]
    return jnp.where(live_mask[None], picked, filler)


def pair_force(first_cols, second):
    separation = first_cols[0:3] - second[0:3]
    distance = jnp.sqrt(jnp.sum(separation * separation, axis=0))
    normal = separation / jnp.maximum(distance, FLOOR)
    intersection = jnp.maximum(first_cols[6] + second[6] - distance, 0.0)
    closing = jnp.sum((first_cols[3:6] - second[3:6]) * normal, axis=0)
    root_intersection = jnp.sqrt(intersection)
    magnitude = STIFF * intersection * root_intersection - DAMPING * root_intersection * closing
    return magnitude * normal


def coupling_terms(state):
    radius = state[6]
    drag_rate = BETA_RATE * radius
    return jnp.concatenate(
        [(VOLUME * radius**3)[None], drag_rate[None], drag_rate[None] * state[3:6]], axis=0
    )


def advance(state, forces, gas_cells, cells):
    at_cell = jnp.take(gas_cells, cells, axis=1)
    velocity = state[3:6]
    drag_rate = BETA_RATE * state[6]
    gravity = jnp.array([0.0, 0.0, -GRAVITY], state.dtype)[:, None]
    return (
        velocity
        + TIME_STEP * (forces + drag_rate * (at_cell - velocity)) / state[7]
        + TIME_STEP * gravity
    )


def on_device(
    particle_state,
    particle_cell,
    boundary_list,
    boundary_count,
    contact_own,
    contact_other,
    contact_count,
    gas_velocity,
    gas_source,
):
    my_half = lax.axis_index("solver")
    halves = lax.axis_size("solver")
    own_count = particle_state.shape[1]
    list_width = boundary_list.shape[-1]
    quadrants = pick_quadrants(
        particle_state, boundary_list.reshape(2, 2, list_width), boundary_count.reshape(2, 2)
    )
    grown_grid = extended(quadrants, (("tx", 1), ("ty", 2)), 1)
    slot_list, offsets = cycle_layout()
    cycle_cols = grown_grid.reshape(8, 16, list_width)[:, slot_list, :] + jnp.asarray(offsets)
    cycle_cols = cycle_cols.reshape(8, 12 * list_width)
    tile_own, tile_cycle = (
        lax.all_gather(particle_state, "solver", axis=1, tiled=True),
        lax.all_gather(cycle_cols, "solver", axis=1, tiled=True),
    )
    tile_data = jnp.concatenate([tile_own, tile_cycle], axis=1)
    gas_tile = lax.all_gather(gas_velocity, "solver", axis=1, tiled=True).reshape(3, -1)
    own_pairs = contact_own.reshape(-1)
    other_pairs = contact_other.reshape(-1)
    live_count = contact_count.reshape(())
    pair_total = own_pairs.shape[0]
    block_len = min(1024, pair_total)
    rounds = (live_count + block_len - 1) // block_len
    own_offset = my_half * own_count

    def add_block(round_index, forces):
        start = round_index * block_len
        own_rows = lax.dynamic_slice_in_dim(own_pairs, start, block_len)
        other_rows = lax.dynamic_slice_in_dim(other_pairs, start, block_len)
        live_mask = (start + jnp.arange(block_len, dtype=jnp.int32) < live_count).astype(
            jnp.float32
        )
        first_cols = jnp.take(tile_data, own_offset + own_rows, axis=1)
        second = jnp.take(tile_data, other_rows, axis=1)
        return forces.at[:, own_rows].add(pair_force(first_cols, second) * live_mask)

    forces = lax.fori_loop(0, rounds, add_block, jnp.zeros((3, own_count), jnp.float32))
    particle_velocity = advance(particle_state, forces, gas_tile, particle_cell)
    levels, rows_x, rows_y = (gas_velocity.shape[1], gas_velocity.shape[2], gas_velocity.shape[3])
    cells_dev = levels * rows_x * rows_y
    binned = (
        jnp.zeros((5, halves * cells_dev), jnp.float32)
        .at[:, particle_cell]
        .add(coupling_terms(particle_state))
    )
    coupled = lax.psum_scatter(binned, "solver", scatter_dimension=1, tiled=True)
    coupled = coupled.reshape(5, levels, rows_x, rows_y)
    porous = 1.0 / (1.0 + coupled[0])
    rhs_gas = porous * gas_velocity + coupled[2:5] + gas_source
    diagonal = porous + coupled[1] + 6.0 * VISCOSITY
    lower_keep = (my_half > 0).astype(jnp.float32)
    upper_keep = (my_half < halves - 1).astype(jnp.float32)

    def sweep(sweep_index, gas_field):
        padded = extended(gas_field, (("tx", 2), ("ty", 3), ("solver", 1)), 1)
        padded = jnp.concatenate(
            [padded[:, :1] * lower_keep, padded[:, 1:-1], padded[:, -1:] * upper_keep], axis=1
        )
        beside = padded[:, 2:, 1:-1, 1:-1] + padded[:, :-2, 1:-1, 1:-1]
        beside = beside + padded[:, 1:-1, 2:, 1:-1] + padded[:, 1:-1, :-2, 1:-1]
        beside = beside + padded[:, 1:-1, 1:-1, 2:] + padded[:, 1:-1, 1:-1, :-2]
        return (rhs_gas + VISCOSITY * beside) / diagonal

    gas_field = lax.fori_loop(0, ITERS, sweep, gas_velocity)
    return (particle_velocity, gas_field)


def solution(mesh):
    in_specs = (
        P(None, ("tx", "ty", "solver")),
        P(("tx", "ty", "solver")),
        P("tx", "ty", "solver", None, None, None),
        P("tx", "ty", "solver", None, None),
        P("tx", "ty", "solver", None),
        P("tx", "ty", "solver", None),
        P("tx", "ty", "solver"),
        P(None, "solver", "tx", "ty"),
        P(None, "solver", "tx", "ty"),
    )
    out_specs = (P(None, ("tx", "ty", "solver")), P(None, "solver", "tx", "ty"))
    return jax.shard_map(
        on_device, mesh=mesh, in_specs=in_specs, out_specs=out_specs, check_vma=False
    )
```

profile of v0, /device:TPU:0, one launch (start us, length us, event | category | flops | bytes accessed | tf_op | source)
XLA Modules:
  0.0 776.5 jit_solution(12515447778052277340)
XLA Ops:
  21.2 6.7 all_gather.9
  36.0 16.4 %gather_fusion.4 = f32[4096,3]{1,0:T(8,128)} fusion(f32[3,8192]{0,1:T(8,128)} %bitcast.64, s32[4096]{0:T(1024)S(1)} %get-tuple-element.157), kind=kCustom, calls=%fused_computation.4 | custom fusion | bytes 114688 | tf_op jit(solution)/shard_map/jit(_take)/gather | solution.py:81
  63.3 176.8 %while.20 = (s32[]{:T(128)}, f32[3,4096]{0,1:T(8,128)S(1)}, s32[]{:T(128)}, s32[16384]{0:T(1024)}, s32[]{:T(128)}, /*index=5*/f32[8,14336]{0,1:T(8,128)}, s32[16...) while((s32[]{:T(128)}, f32[3,4096]{0,1:T(8,128)S(1)}, s32[]{:T(128)}, ...), condition=%wide.region_4.6_spmd, body=%wide.region_0.5_spmd.sunk | while | flops 91142 | bytes 671935 | solution.py:139
  64.1 5.9 gather_fusion
  71.5 5.9 gather_fusion.1
  78.6 6.8 scatter_fusion
  93.6 5.9 gather_fusion.1
  100.7 6.8 scatter_fusion
  115.7 5.9 gather_fusion.1
  122.8 6.8 scatter_fusion
  130.4 5.9 gather_fusion
  137.8 5.9 gather_fusion.1
  144.9 6.8 scatter_fusion
  167.0 6.8 scatter_fusion
  174.6 5.9 gather_fusion
  189.1 6.8 scatter_fusion
  196.6 5.9 gather_fusion
  211.2 6.8 scatter_fusion
  218.7 5.9 gather_fusion
  233.3 6.8 scatter_fusion
  240.1 7.0 slice_multiply_fusion
  250.1 24.6 %scatter_custom_fusion.1 = f32[5,8192]{0,1:T(8,128)} fusion(s32[4096]{0:T(1024)S(1)} %get-tuple-element.156, f32[4096,5]{1,0:T(8,128)S(1)} %copy.52, f32[]{:T(128)} %constant.52.clone.1), kind=kCustom, calls=%fused_computation.72 | custom fusion | flops 20480 | bytes 163844 | tf_op jit(solution)/shard_map/scatter-add | solution.py:146
  277.5 227.5 %reduce-scatter.2.cloned.1.call-done = f32[5,4096]{0,1:T(8,128)} async-done(((f32[5,8192]{0,1:T(8,128)}), f32[5,4096]{0,1:T(8,128)}) %reduce-scatter.2.cloned.1.call-update) | async-done | bytes 81936 | tf_op jit(solution)/shard_map/reduce_scatter | solution.py:148
  512.6 256.4 %while.21 = (s32[]{:T(128)}, f32[3,8,4,128]{3,2,1,0:T(4,128)S(1)}, f32[]{:T(128)}, f32[]{:T(128)}, f32[3,8,4,128]{3,2,1,0:T(4,128)S(1)}, /*index=5*/f32[8,4,128]{2,1,0:T(4,128)S(1)}, s32[]{:T(128)}) while((s32[]{:T(128)}, f32[3,8,4,128]{3,2,1,0:T(4,128)S(1)}, f32[]{:T(128)}, f32[]{:T(128)}, f32[3,8,4,128]{3,2,1,0:T(4,128)S(1)}, ...), condition=%wide.region_8.10_spmd, body=%wide.region_7.9_spmd.sunk | while | flops 367466 | bytes 814661 | solution.py:166
  (501 shorter events, 370.2 us)
Async XLA Ops:
  7.2 497.8 %reduce-scatter.2.cloned.1.call-start = ((), (), s32[]{:S(2)}) async-start(), calls=%async_computation.1 | async-start | bytes 6291456 | tf_op jit(solution)/shard_map/reduce_scatter | solution.py:148
  16.7 35.7 %collective-permute-start.8 = (f32[8,4,1,256]{3,0,2,1:T(8,128)S(1)}, f32[8,4,1,256]{3,0,2,1:T(8,128)S(1)}, u32[]{:S(2)}, u32[]{:S(2)}) collective-permute-start(f32[8,4,1,256]{3,0,2,1:T(8,128)S(1)} %get-tuple-element.152), channel_id=1, source_target_pairs={{0,2},{2,4},{4,6},{6,0},{1,3},{3,5},{5,7},{7,1},{8,10},{10,12},{12... | collective-permute-start | bytes 98312 | tf_op jit(solution)/shard_map/ppermute | solution.py:27
  19.1 33.3 %collective-permute-start.9 = (f32[8,4,1,256]{3,0,2,1:T(8,128)S(1)}, f32[8,4,1,256]{3,0,2,1:T(8,128)S(1)}, u32[]{:S(2)}, u32[]{:S(2)}) collective-permute-start(f32[8,4,1,256]{3,0,2,1:T(8,128)S(1)} %get-tuple-element.153), channel_id=1, source_target_pairs={{2,0},{4,2},{6,4},{0,6},{3,1},{5,3},{7,5},{1,7},{10,8},{12,10},{14... | collective-permute-start | bytes 98312 | tf_op jit(solution)/shard_map/ppermute | solution.py:30
  516.9 6.8 collective-permute-start.2
  532.4 7.5 collective-permute-start.2
  533.6 6.6 collective-permute-start.3
  549.5 7.1 collective-permute-start.2
  550.3 6.3 collective-permute-start.3
  564.9 7.2 collective-permute-start.2
  566.1 6.0 collective-permute-start.3
  581.3 7.1 collective-permute-start.2
  582.4 6.1 collective-permute-start.3
  596.8 7.0 collective-permute-start.2
  613.1 7.2 collective-permute-start.2
  628.6 7.0 collective-permute-start.2
  645.1 7.0 collective-permute-start.2
  660.4 7.2 collective-permute-start.2
  676.9 7.0 collective-permute-start.2
  678.0 6.0 collective-permute-start.3
  692.4 7.0 collective-permute-start.2
  708.7 7.2 collective-permute-start.2
  724.2 7.0 collective-permute-start.2
  740.6 7.0 collective-permute-start.2
  756.0 7.2 collective-permute-start.2
  (90 other events, 537.7 us)
Sparse Core Ops, SparseCore 0:
  274.8 230.1 reduce-scatter.1
where the time goes:
time: 780 us; the launch traced here: 776 us
  waiting for transfers between devices  370 us (47%)
  local copies, waits for them, and re-layouts  142 us (18%)
  other arithmetic  119 us (15%)
  starting transfers between devices  112 us (14%)
  blocking collectives  16.8 us (2%)
  between operations  15 us (2%)
    reduce_scatter x1, waiting for transfers between devices, on_device(): lax.psum_scatter(binned, 'solver', scatter_dimension=1, tiled=True)  227 us
    ppermute x50, waiting for transfers between devices, extended(): lax.ppermute(lax.slice_in_dim(block, block.shape[dim] - width, None, axis...  110 us
    ppermute x50, starting transfers between devices, extended(): lax.ppermute(lax.slice_in_dim(block, 0, width, axis=dim), axis, backward)  64.8 us
    scatter-add x8, other arithmetic, add_block(): forces.at[:, own_rows].add(pair_force(first_cols, second) * live_mask)  54.4 us
    gather x16, local copies, waits for them, and re-layouts, add_block(): second = jnp.take(tile_data, other_rows, axis=1)  48.4 us
    gather x16, local copies, waits for them, and re-layouts, add_block(): first_cols = jnp.take(tile_data, own_offset + own_rows, axis=1)  48.4 us
    ppermute x50, starting transfers between devices, extended(): lax.ppermute(lax.slice_in_dim(block, block.shape[dim] - width, None, axis...  46.9 us
    ppermute x50, waiting for transfers between devices, extended(): lax.ppermute(lax.slice_in_dim(block, 0, width, axis=dim), axis, backward)  33.2 us
  transfers between devices with their start and end apart: 101, of which 93 were waited for; matrix products, arithmetic and copies ran while one was open for 3% of the time, Pallas kernels for 0%

commit v1 on v0

v1 whole, which is shorter than its diff:
```python
import functools

import jax
import jax.numpy as jnp
from jax import lax
from jax.experimental import pallas as pl
from jax.experimental.pallas import tpu as pltpu
from jax.sharding import PartitionSpec as P

ITERS = 16
FAR = 100.0
STIFF = 4.0
DAMPING = 1.0
FLOOR = 0.1
BETA_RATE = 2.0
VOLUME = 4.18879
TIME_STEP = 0.1
GRAVITY = 1.0
VISCOSITY = 1.0
SUB = 8
LANES = 128
HALO = 16
PAIR_ROWS = 32
SHIFTS = (-1, 0, 0, 1)
SLOTS = tuple((a, b) for a in range(4) for b in range(4) if not (a in (1, 2) and b in (1, 2)))
VMEM_LIMIT = 48 << 20
MESH = pl.DeviceIdType.MESH
F32 = jnp.float32


def vmem_specs(count):
    return [pl.BlockSpec(memory_space=pltpu.VMEM)] * count


def lane_take(row, low):
    return jnp.take_along_axis(jnp.broadcast_to(row, low.shape), low, axis=1, mode="promise_in_bounds")


def take_groups(load_row, rows, groups, high, low, unroll):
    chunks = high[0].shape
    start = tuple(jnp.zeros(chunks, F32) for _ in range(len(high) * len(rows)))

    def step(group, acc):
        out = []
        table = [load_row(r, group) for r in rows]
        for i in range(len(high)):
            hit = high[i] == group
            for j in range(len(rows)):
                out.append(jnp.where(hit, lane_take(table[j], low[i]), acc[i * len(rows) + j]))
        return tuple(out)

    flat = lax.fori_loop(0, groups, step, start, unroll=unroll)
    return [flat[i * len(rows) : (i + 1) * len(rows)] for i in range(len(high))]


def two_parts(value):
    high = value.astype(jnp.bfloat16).astype(F32)
    return (high, value - high)


def spread_dot(values, high, low, high_count):
    row_count = high.shape[0]
    parts = []
    for value in values:
        parts.extend(two_parts(value))
    lefts = []
    rights = []
    high_iota = lax.broadcasted_iota(jnp.int32, (high_count, LANES), 0)
    low_iota = lax.broadcasted_iota(jnp.int32, (LANES, LANES), 0)
    for s in range(row_count):
        hit = jnp.broadcast_to(high[s : s + 1], (high_count, LANES)) == high_iota
        left = [
            jnp.where(hit, jnp.broadcast_to(part[s : s + 1], (high_count, LANES)), 0.0).astype(jnp.bfloat16)
            for part in parts
        ]
        lefts.append(jnp.concatenate(left, axis=0))
        right = jnp.broadcast_to(low[s : s + 1], (LANES, LANES)) == low_iota
        rights.append(jnp.where(right, 1.0, 0.0).astype(jnp.bfloat16))
    left = jnp.concatenate(lefts, axis=1)
    right = jnp.concatenate(rights, axis=1)
    out = lax.dot_general(left, right, (((1,), (1,)), ((), ())), preferred_element_type=F32)
    sums = []
    for i in range(len(values)):
        base = 2 * i * high_count
        sums.append(out[base : base + high_count] + out[base + high_count : base + 2 * high_count])
    return sums


def pack_edges(rows):
    lane = lax.broadcasted_iota(jnp.int32, rows[0].shape, 1)
    half = LANES // 2
    packed = jnp.zeros(rows[0].shape, F32)
    for x, row in enumerate(rows):
        left = pltpu.roll(row, (x * HALO) % LANES, axis=1)
        right = pltpu.roll(row, (half + x * HALO + HALO) % LANES, axis=1)
        packed = jnp.where((lane >= x * HALO) & (lane < x * HALO + HALO), left, packed)
        base = half + x * HALO
        packed = jnp.where((lane >= base) & (lane < base + HALO), right, packed)
    return packed


def local_kernel(
    levels_all, rows_x,
    count_ref, state_ref, cell_ref, list_ref, gas_ref, source_ref,
    ghost_ref, bins_ref, field_ref, src_ref, edge_ref,
):
    groups = state_ref.shape[1] // LANES
    index = list_ref[...]
    picked = take_groups(
        lambda r, g: state_ref[r : r + 1, pl.ds(pl.multiple_of(g * LANES, LANES), LANES)],
        range(8), groups, [index >> 7], [index & 127], 4,
    )[0]
    lines = index.shape[0] // 4
    row_iota = lax.broadcasted_iota(jnp.int32, index.shape, 0)
    place = (row_iota % lines) * LANES + lax.broadcasted_iota(jnp.int32, index.shape, 1)
    quad = row_iota // lines
    limit = jnp.zeros(index.shape, jnp.int32)
    for q in range(4):
        limit = jnp.where(quad == q, count_ref[q], limit)
    live = place < limit
    width = lines * LANES
    for r in range(8):
        value = jnp.where(live, picked[r], FAR if r < 3 else 0.0)
        for s, (a, b) in enumerate(SLOTS):
            q = ((a + 1) % 2) * 2 + (b + 1) % 2
            shift = SHIFTS[a] if r == 0 else SHIFTS[b] if r == 1 else 0
            for line in range(lines):
                row = value[q * lines + line : q * lines + line + 1]
                if r < 2:
                    row = row + float(shift)
                base = s * width + line * LANES
                ghost_ref[r : r + 1, base : base + LANES] = row

    high_count = rows_x * levels_all
    totals = None
    for block in range(groups // SUB):
        rows = [
            jnp.concatenate(
                [
                    state_ref[r : r + 1, (block * SUB + s) * LANES : (block * SUB + s + 1) * LANES]
                    for s in range(SUB)
                ],
                axis=0,
            )
            for r in (3, 4, 5, 6)
        ]
        radius = rows[3]
        drag = BETA_RATE * radius
        values = [VOLUME * radius * radius * radius, drag] + [drag * rows[c] for c in range(3)]
        cell = cell_ref[block * SUB : (block + 1) * SUB, :]
        line = cell >> 7
        high = (line % rows_x) * levels_all + line // rows_x
        sums = spread_dot(values, high, cell & 127, high_count)
        totals = sums if totals is None else [t + s for t, s in zip(totals, sums)]
    for p in range(5):
        bins_ref[p] = totals[p].reshape(rows_x, levels_all, LANES)
    for c in range(3):
        rows = []
        for x in range(rows_x):
            row = gas_ref[c, :, x, :]
            rows.append(row)
            field_ref[c, x] = row
            src_ref[c, x] = source_ref[c, :, x, :]
        edge_ref[c] = pack_edges(rows)


def exchange_kernel(
    sizes,
    state_ref, ghost_ref, bins_ref, field_ref, src_ref, edge_ref,
    tile_ref, gas_all, rhs_all, above_gas, below_gas, above_rhs, below_rhs,
    bins_in, mine, mine_edge, send_sem, recv_sem,
):
    n_x, n_y, n_h = sizes
    x, y, h = (lax.axis_index(name) for name in ("tx", "ty", "solver"))
    levels = field_ref.shape[2]
    rows_x = field_ref.shape[1]
    own = state_ref.shape[1]
    ring = n_x * n_h
    me = x * n_h + h
    barrier = pltpu.get_barrier_semaphore()
    up = (y + 1) % n_y
    down = (y + n_y - 1) % n_y

    def member(step):
        spot = (me + step) % ring
        return spot // n_h, spot % n_h

    for step in range(ring):
        t, k = member(step)
        for line in ((y, up, down) if step else (up, down)):
            pl.semaphore_signal(barrier, inc=1, device_id=(t, line, k), device_id_type=MESH)
    pl.semaphore_wait(barrier, 3 * ring - 1)

    copies = []

    def send(src, dst, kind, target):
        copy = pltpu.make_async_remote_copy(
            src_ref=src, dst_ref=dst, send_sem=send_sem.at[len(copies)], recv_sem=recv_sem.at[kind],
            device_id=target, device_id_type=MESH,
        )
        copy.start()
        copies.append(copy)

    def keep(src, dst, kind):
        pltpu.make_async_copy(src, dst, recv_sem.at[kind]).start()

    partner = (h + 1) % n_h
    theirs = pl.multiple_of(partner * levels, levels)
    here = pl.multiple_of(h * levels, levels)
    send(bins_ref.at[:, :, pl.ds(theirs, levels), :], bins_in, 0, (x, y, partner))
    state_at = tile_ref.at[:, pl.ds(pl.multiple_of(h * own, own), own)]
    send(state_ref, state_at, 1, (x, y, partner))
    keep(state_ref, state_at, 1)
    cycle = ghost_ref.shape[1]
    width = cycle // len(SLOTS)
    base = n_h * own + h * cycle
    runs = ((0, 1), (1, 2), (3, 1), (4, 1), (5, 1), (6, 1), (7, 1), (8, 1), (9, 2), (11, 1))
    for first, length in runs:
        a, b = SLOTS[first]
        to_x = (x + n_x - SHIFTS[a]) % n_x
        to_y = (y + n_y - SHIFTS[b]) % n_y
        src = ghost_ref.at[:, first * width : (first + length) * width]
        dst = tile_ref.at[:, pl.ds(pl.multiple_of(base + first * width, width), length * width)]
        for k in range(n_h):
            send(src, dst, 1, (to_x, to_y, (h + k) % n_h))

    def gather(block, edges, whole, above, below, kinds):
        spot = whole.at[:, pl.ds(x * rows_x, rows_x), pl.ds(here, levels), :]
        keep(block, spot, kinds)
        for step in range(1, ring):
            t, k = member(step)
            send(block, spot, kinds, (t, y, k))
        for step in range(ring):
            t, k = member(step)
            send(edges, above.at[:, x, pl.ds(here, levels), :], kinds + 1, (t, down, k))
            send(edges, below.at[:, x, pl.ds(here, levels), :], kinds + 2, (t, up, k))

    gather(field_ref, edge_ref, gas_all, above_gas, below_gas, 2)
    pltpu.make_async_copy(bins_in, bins_in, recv_sem.at[0]).wait()
    edge_rows = [[], [], [], []]
    for i in range(rows_x):
        sums = [bins_ref[p, i, pl.ds(here, levels), :] + bins_in[p, i] for p in range(5)]
        porous = 1.0 / (1.0 + sums[0])
        inverse = 1.0 / (porous + sums[1] + 6.0 * VISCOSITY)
        values = [porous * field_ref[c, i] + sums[2 + c] + src_ref[c, i] for c in range(3)] + [inverse]
        for p in range(4):
            mine[p, i] = values[p]
            edge_rows[p].append(values[p])
    for p in range(4):
        mine_edge[p] = pack_edges(edge_rows[p])
    gather(mine, mine_edge, rhs_all, above_rhs, below_rhs, 5)
    for kind, ref in enumerate((tile_ref, gas_all, above_gas, below_gas, rhs_all, above_rhs, below_rhs)):
        pltpu.make_async_copy(ref, ref, recv_sem.at[kind + 1]).wait()
    for copy in copies:
        copy.wait_send()


def pair_kernel(
    rows_x,
    count_ref, tile_ref, state_ref, state_rows, cell_ref, own_ref, other_ref, gas_all,
    out_ref, force_ref,
):
    levels_all = gas_all.shape[2]
    x = lax.axis_index("tx")
    groups = state_ref.shape[1] // LANES
    tile_groups = tile_ref.shape[1] // LANES
    force_ref[...] = jnp.zeros_like(force_ref)
    count = count_ref[0]
    block = PAIR_ROWS * LANES
    chunks = PAIR_ROWS // SUB

    @pl.loop(0, (count + block - 1) // block)
    def _(round_index):
        start = pl.multiple_of(round_index * PAIR_ROWS, PAIR_ROWS)
        own = [own_ref[pl.ds(start + i * SUB, SUB), :] for i in range(chunks)]
        other = [other_ref[pl.ds(start + i * SUB, SUB), :] for i in range(chunks)]
        rows = range(7)
        first = take_groups(
            lambda r, g: state_ref[r : r + 1, pl.ds(pl.multiple_of(g * LANES, LANES), LANES)],
            rows, groups, [v >> 7 for v in own], [v & 127 for v in own], 2,
        )
        second = take_groups(
            lambda r, g: tile_ref[r : r + 1, pl.ds(pl.multiple_of(g * LANES, LANES), LANES)],
            rows, tile_groups, [v >> 7 for v in other], [v & 127 for v in other], 2,
        )
        for i in range(chunks):
            a, b = first[i], second[i]
            gap = [a[c] - b[c] for c in range(3)]
            distance = jnp.sqrt(gap[0] * gap[0] + gap[1] * gap[1] + gap[2] * gap[2])
            scale = 1.0 / jnp.maximum(distance, FLOOR)
            normal = [v * scale for v in gap]
            overlap = jnp.maximum(a[6] + b[6] - distance, 0.0)
            closing = sum((a[3 + c] - b[3 + c]) * normal[c] for c in range(3))
            root = jnp.sqrt(overlap)
            size = STIFF * overlap * root - DAMPING * root * closing
            place = (
                (start + i * SUB + lax.broadcasted_iota(jnp.int32, (SUB, LANES), 0)) * LANES
                + lax.broadcasted_iota(jnp.int32, (SUB, LANES), 1)
            )
            size = jnp.where(place < count, size, 0.0)
            sums = spread_dot([size * v for v in normal], own[i] >> 7, own[i] & 127, groups)
            for c in range(3):
                force_ref[c] += sums[c]

    for i in range(groups // SUB):
        cell = cell_ref[i * SUB : (i + 1) * SUB, :]
        line = cell >> 7
        high = (line % rows_x) * levels_all + line // rows_x
        at_cell = take_groups(
            lambda c, g: gas_all[c, x * rows_x + g // levels_all, pl.ds(g % levels_all, 1), :],
            range(3), rows_x * levels_all, [high], [cell & 127], 4,
        )[0]
        span = slice(i * SUB, (i + 1) * SUB)
        drag = BETA_RATE * state_rows[6, span, :]
        rate = TIME_STEP / state_rows[7, span, :]
        for c in range(3):
            velocity = state_rows[3 + c, span, :]
            value = velocity + (force_ref[c, span, :] + drag * (at_cell[c] - velocity)) * rate
            if c == 2:
                value = value - TIME_STEP * GRAVITY
            out_ref[c, span, :] = value


def sweep_kernel(
    rows_x,
    gas_all, rhs_all, above_gas, below_gas, above_rhs, below_rhs,
    out_ref, field_a, field_b, rhs_ref,
):
    n_all, levels_all = gas_all.shape[1], gas_all.shape[2]
    levels = out_ref.shape[1]
    x, h = lax.axis_index("tx"), lax.axis_index("solver")
    lane = lax.broadcasted_iota(jnp.int32, (levels_all, LANES), 1)

    def fill(planes, whole, above, below, target):
        @pl.loop(0, n_all // rows_x)
        def _(t):
            for p in range(planes):
                high = above[p, t]
                low = below[p, t]
                for i in range(rows_x):
                    at = t * rows_x + i
                    target[p, at, :, 0:LANES] = whole[p, at]
                    right = pltpu.roll(high, (LANES - i * HALO) % LANES, axis=1)
                    left = pltpu.roll(low, (LANES // 2 - (i + 1) * HALO) % LANES, axis=1)
                    edge = jnp.where(lane < HALO, right, jnp.where(lane >= LANES - HALO, left, 0.0))
                    target[p, at, :, LANES : 2 * LANES] = edge

    fill(3, gas_all, above_gas, below_gas, field_a)
    fill(4, rhs_all, above_rhs, below_rhs, rhs_ref)
    level = lax.broadcasted_iota(jnp.int32, (levels_all, 2 * LANES), 0)

    def sweep(source, target):
        @pl.loop(0, n_all // 2)
        def _(pair):
            for j in range(2):
                at = pair * 2 + j
                inverse = rhs_ref[3, at]
                for c in range(3):
                    mid = source[c, at]
                    total = rhs_ref[c, at] + source[c, (at + 1) % n_all] + source[c, (at + n_all - 1) % n_all]
                    total = total + jnp.where(level == 0, 0.0, pltpu.roll(mid, 1, axis=0))
                    total = total + jnp.where(level == levels_all - 1, 0.0, pltpu.roll(mid, levels_all - 1, axis=0))
                    total = total + pltpu.roll(mid, 1, axis=1) + pltpu.roll(mid, 2 * LANES - 1, axis=1)
                    target[c, at] = total * inverse

    @pl.loop(0, ITERS // 2)
    def _(step):
        sweep(field_a, field_b)
        sweep(field_b, field_a)

    here = pl.multiple_of(h * levels, levels)
    for c in range(3):
        for i in range(rows_x):
            out_ref[c, :, i, :] = field_a[c, x * rows_x + i, pl.ds(here, levels), 0:LANES]


def on_device(
    sizes,
    particle_state, particle_cell, boundary_list, boundary_count,
    contact_own, contact_other, contact_count, gas_velocity, gas_source,
):
    n_x, n_y, n_h = sizes
    own = particle_state.shape[1]
    levels, rows_x, rows_y = gas_velocity.shape[1:]
    levels_all = levels * n_h
    width = boundary_list.shape[-1]
    cycle = len(SLOTS) * width
    shape = lambda *dims: jax.ShapeDtypeStruct(dims, F32)
    smem = pl.BlockSpec(memory_space=pltpu.SMEM)
    params = functools.partial(pltpu.CompilerParams, vmem_limit_bytes=VMEM_LIMIT)
    cells = particle_cell.reshape(-1, LANES)
    ghosts, bins, field, source, edges = pl.pallas_call(
        functools.partial(local_kernel, levels_all, rows_x),
        out_shape=(
            shape(8, cycle), shape(5, rows_x, levels_all, rows_y), shape(3, rows_x, levels, rows_y),
            shape(3, rows_x, levels, rows_y), shape(3, levels, LANES),
        ),
        in_specs=[smem] + vmem_specs(5),
        out_specs=tuple(vmem_specs(5)),
        compiler_params=params(),
        name="local",
    )(
        boundary_count.reshape(4), particle_state, cells, boundary_list.reshape(-1, LANES),
        gas_velocity, gas_source,
    )
    n_all = n_x * rows_x
    ring = n_x * n_h
    sends = 2 + 10 * n_h + 2 * (ring - 1 + 2 * ring)
    tile, gas_all, rhs_all, above_gas, below_gas, above_rhs, below_rhs = pl.pallas_call(
        functools.partial(exchange_kernel, sizes),
        out_shape=(
            shape(8, n_h * (own + cycle)),
            shape(3, n_all, levels_all, rows_y), shape(4, n_all, levels_all, rows_y),
            shape(3, n_x, levels_all, LANES), shape(3, n_x, levels_all, LANES),
            shape(4, n_x, levels_all, LANES), shape(4, n_x, levels_all, LANES),
        ),
        in_specs=vmem_specs(6),
        out_specs=tuple(vmem_specs(7)),
        scratch_shapes=[
            pltpu.VMEM((5, rows_x, levels, rows_y), F32),
            pltpu.VMEM((4, rows_x, levels, rows_y), F32),
            pltpu.VMEM((4, levels, LANES), F32),
            pltpu.SemaphoreType.DMA((sends,)),
            pltpu.SemaphoreType.DMA((8,)),
        ],
        compiler_params=params(collective_id=0, has_side_effects=True),
        name="exchange",
    )(particle_state, ghosts, bins, field, source, edges)
    moved = pl.pallas_call(
        functools.partial(pair_kernel, rows_x),
        out_shape=shape(3, own // LANES, LANES),
        in_specs=[smem] + vmem_specs(7),
        out_specs=vmem_specs(1)[0],
        scratch_shapes=[pltpu.VMEM((3, own // LANES, LANES), F32)],
        compiler_params=params(),
        name="pairs",
    )(
        contact_count.reshape(1), tile, particle_state, particle_state.reshape(8, -1, LANES), cells,
        contact_own.reshape(-1, LANES), contact_other.reshape(-1, LANES), gas_all,
    )
    swept = pl.pallas_call(
        functools.partial(sweep_kernel, rows_x),
        out_shape=shape(3, levels, rows_x, rows_y),
        in_specs=vmem_specs(6),
        out_specs=vmem_specs(1)[0],
        scratch_shapes=[
            pltpu.VMEM((3, n_all, levels_all, 2 * LANES), F32),
            pltpu.VMEM((3, n_all, levels_all, 2 * LANES), F32),
            pltpu.VMEM((4, n_all, levels_all, 2 * LANES), F32),
        ],
        compiler_params=params(),
        name="sweeps",
    )(gas_all, rhs_all, above_gas, below_gas, above_rhs, below_rhs)
    return (moved.reshape(3, own), swept)


def solution(mesh):
    sizes = (mesh.shape["tx"], mesh.shape["ty"], mesh.shape["solver"])
    in_specs = (
        P(None, ("tx", "ty", "solver")),
        P(("tx", "ty", "solver")),
        P("tx", "ty", "solver", None, None, None),
        P("tx", "ty", "solver", None, None),
        P("tx", "ty", "solver", None),
        P("tx", "ty", "solver", None),
        P("tx", "ty", "solver"),
        P(None, "solver", "tx", "ty"),
        P(None, "solver", "tx", "ty"),
    )
    out_specs = (P(None, ("tx", "ty", "solver")), P(None, "solver", "tx", "ty"))
    return jax.shard_map(
        functools.partial(on_device, sizes), mesh=mesh, in_specs=in_specs, out_specs=out_specs, check_vma=False
    )
```

time: 780 us -> 108 us (0.14)
  the two profiles are of different devices: /device:TPU:0 before, /device:TPU:4 now
where the time goes in v1:
time: 108 us
  Pallas kernels  101 us (94%)
  local copies, waits for them, and re-layouts  4.86 us (5%)
  between operations  1.35 us (1%)
    pallas_call x1, Pallas kernels, on_device(): pl.pallas_call(functools.partial(pair_kernel, rows_x), out_shape=shape(3,...  52.4 us
    pallas_call x1, Pallas kernels, on_device(): pl.pallas_call(functools.partial(exchange_kernel, sizes), out_shape=(shap...  28.8 us
    pallas_call x1, Pallas kernels, on_device(): pl.pallas_call(functools.partial(sweep_kernel, rows_x), out_shape=shape(3...  17.2 us
    unnamed x18, local copies, waits for them, and re-layouts  4.08 us
    pallas_call x1, Pallas kernels, on_device(): pl.pallas_call(functools.partial(local_kernel, levels_all, rows_x), out_s...  2.9 us

profile of v1, /device:TPU:4, one launch (start us, length us, event | category | flops | bytes accessed | tf_op | source)
XLA Modules:
  0.0 107.5 jit_solution(374387597098486684)
XLA Ops:
  0.6 0.0 copy-start.7
  0.6 0.7 reshape.31.list_ref
  1.3 0.0 copy-done.7
  1.3 0.1 reshape.29.count_ref
  1.4 0.0 copy-start
  1.4 0.9 copy-done
  2.3 0.0 copy-start.2
  2.3 0.7 copy-done.2
  3.0 0.0 copy-start.5
  3.1 0.8 copy-done.5
  3.8 0.0 copy-start.6
  3.8 0.8 copy-done.6
  4.6 0.0 copy-start.1
  4.6 2.9 %local.1 = (f32[8,3072]{1,0:T(8,128)S(1)}, f32[5,4,16,128]{3,2,1,0:T(8,128)S(1)}, f32[3,4,8,128]{3,2,1,0:T(8,128)S(1)}, f32[3,4,8,128]{3,2,1,0:T(8,128)S(1)}, f32[3,8,128]{2,1,0:T(8,128)S(1)}) custom-call(s32[4]{0:T(128)S(1)} %reshape.29.count_ref, f32[8,4096]{1,0:T(8,128)S(1)} %copy-done, s32[32,128]{1,0:T(8,128)S(1)} %bitcast.16, ...), custom_call_target="tpu_custom_call" | custom-call | tf_op jit(solution)/shard_map/local/pallas_call | solution.py:392
  7.6 0.0 copy-done.1
  7.6 28.8 %exchange.1 = (f32[8,14336]{1,0:T(8,128)S(1)}, f32[3,16,16,128]{3,2,1,0:T(8,128)S(1)}, f32[4,16,16,128]{3,2,1,0:T(8,128)S(1)}, f32[3,4,16,128]{3,2,1,0:T(8,128)S...) custom-call(f32[8,4096]{1,0:T(8,128)S(1)} %copy-done.1, ...), custom_call_target="tpu_custom_call" | custom-call | tf_op jit(solution)/shard_map/exchange/pallas_call | solution.py:409
  36.3 17.2 %sweeps.1 = f32[3,8,4,128]{3,2,1,0:T(4,128)} custom-call(f32[3,16,16,128]{3,2,1,0:T(8,128)S(1)} %get-tuple-element.20.gas_all, f32[4,16,16,128]{3,2,1,0:T(8,128)S(1)} %get-tuple-element.21.rhs_all, f32[3,4,16,128]{3,2,1,0:T(8,128)S(1)} %get-tuple-element.22.above_gas, f32[3,4,16,128]{3,2,1,0:T(8,128)S(1)} %get-tuple-element.23.below_gas, ...), custom_call_target="tpu_custom_call" | custom-call | tf_op jit(solution)/shard_map/sweeps/pallas_call | solution.py:441
  53.6 0.0 copy-start.3
  53.6 0.0 copy-start.4
  54.3 0.1 copy-done.3
  54.4 0.0 copy-done.4
  54.4 52.4 %pairs.1 = f32[3,32,128]{2,1,0:T(8,128)S(1)} custom-call(s32[1]{0:T(128)} %bitcast.12.count_ref, f32[8,14336]{1,0:T(8,128)S(1)} %get-tuple-element.19.tile_ref, f32[8,4096]{1,0:T(8,128)S(1)} %copy-done.1, f32[8,32,128]{2,1,0:T(8,128)S(1)} %bitcast.14, s32[32,128]{1,0:T(8,128)S(1)} %bitcast.17, s32[128,128]{1,0:T(8,128)S(1)} %bitcast.18, ...), custom_call_target="tpu_custom_call" | custom-call | tf_op jit(solution)/shard_map/pairs/pallas_call | solution.py:429
  106.8 0.7 copy.16
  (1 shorter events, 0.0 us)
Async XLA Ops:
  0.6 0.7 copy-start.7
  1.4 0.9 copy-start
  2.3 0.7 copy-start.2
  3.0 0.8 copy-start.5
  3.8 0.8 copy-start.6
  4.6 2.9 %copy-start.1 = (f32[8,4096]{1,0:T(8,128)S(1)}, f32[8,4096]{1,0:T(8,128)}, u32[]{:S(2)}) copy-start(f32[8,4096]{1,0:T(8,128)} %state_ref.5) | copy-start | bytes 393220
  53.6 0.8 copy-start.3
  53.6 0.9 copy-start.4

commit v2 on v1

--- a/solution.py
+++ b/solution.py
@@ -20,7 +20,6 @@
 SUB = 8
 LANES = 128
 HALO = 16
-PAIR_ROWS = 32
 SHIFTS = (-1, 0, 0, 1)
 SLOTS = tuple((a, b) for a in range(4) for b in range(4) if not (a in (1, 2) and b in (1, 2)))
 VMEM_LIMIT = 48 << 20
@@ -102,7 +101,7 @@
 def local_kernel(
     levels_all, rows_x,
     count_ref, state_ref, cell_ref, list_ref, gas_ref, source_ref,
-    ghost_ref, bins_ref, field_ref, src_ref, edge_ref,
+    ghost_ref, bins_ref, field_ref, src_ref,
 ):
     groups = state_ref.shape[1] // LANES
     index = list_ref[...]
@@ -155,41 +154,33 @@
     for p in range(5):
         bins_ref[p] = totals[p].reshape(rows_x, levels_all, LANES)
     for c in range(3):
-        rows = []
         for x in range(rows_x):
-            row = gas_ref[c, :, x, :]
-            rows.append(row)
-            field_ref[c, x] = row
+            field_ref[c, x] = gas_ref[c, :, x, :]
             src_ref[c, x] = source_ref[c, :, x, :]
-        edge_ref[c] = pack_edges(rows)
 
 
 def exchange_kernel(
     sizes,
-    state_ref, ghost_ref, bins_ref, field_ref, src_ref, edge_ref,
-    tile_ref, gas_all, rhs_all, above_gas, below_gas, above_rhs, below_rhs,
-    bins_in, mine, mine_edge, send_sem, recv_sem,
+    state_ref, ghost_ref, bins_ref, field_ref, src_ref,
+    tile_ref, gas_ref, block_ref,
+    bins_in, edges, above, below, send_sem, recv_sem,
 ):
     n_x, n_y, n_h = sizes
     x, y, h = (lax.axis_index(name) for name in ("tx", "ty", "solver"))
     levels = field_ref.shape[2]
     rows_x = field_ref.shape[1]
     own = state_ref.shape[1]
-    ring = n_x * n_h
-    me = x * n_h + h
     barrier = pltpu.get_barrier_semaphore()
     up = (y + 1) % n_y
     down = (y + n_y - 1) % n_y
-
-    def member(step):
-        spot = (me + step) % ring
-        return spot // n_h, spot % n_h
-
-    for step in range(ring):
-        t, k = member(step)
-        for line in ((y, up, down) if step else (up, down)):
-            pl.semaphore_signal(barrier, inc=1, device_id=(t, line, k), device_id_type=MESH)
-    pl.semaphore_wait(barrier, 3 * ring - 1)
+    partner = (h + 1) % n_h
+    for dx in (0, 1, n_x - 1):
+        for line in (y, up, down):
+            for k in range(n_h):
+                if dx or k or line is not y:
+                    target = ((x + dx) % n_x, line, (h + k) % n_h)
+                    pl.semaphore_signal(barrier, inc=1, device_id=target, device_id_type=MESH)
+    pl.semaphore_wait(barrier, 9 * n_h - 1)
 
     copies = []
 
@@ -201,16 +192,9 @@
         copy.start()
         copies.append(copy)
 
-    def keep(src, dst, kind):
-        pltpu.make_async_copy(src, dst, recv_sem.at[kind]).start()
-
-    partner = (h + 1) % n_h
     theirs = pl.multiple_of(partner * levels, levels)
     here = pl.multiple_of(h * levels, levels)
     send(bins_ref.at[:, :, pl.ds(theirs, levels), :], bins_in, 0, (x, y, partner))
-    state_at = tile_ref.at[:, pl.ds(pl.multiple_of(h * own, own), own)]
-    send(state_ref, state_at, 1, (x, y, partner))
-    keep(state_ref, state_at, 1)
     cycle = ghost_ref.shape[1]
     width = cycle // len(SLOTS)
     base = n_h * own + h * cycle
@@ -223,130 +207,151 @@
         dst = tile_ref.at[:, pl.ds(pl.multiple_of(base + first * width, width), length * width)]
         for k in range(n_h):
             send(src, dst, 1, (to_x, to_y, (h + k) % n_h))
-
-    def gather(block, edges, whole, above, below, kinds):
-        spot = whole.at[:, pl.ds(x * rows_x, rows_x), pl.ds(here, levels), :]
-        keep(block, spot, kinds)
-        for step in range(1, ring):
-            t, k = member(step)
-            send(block, spot, kinds, (t, y, k))
-        for step in range(ring):
-            t, k = member(step)
-            send(edges, above.at[:, x, pl.ds(here, levels), :], kinds + 1, (t, down, k))
-            send(edges, below.at[:, x, pl.ds(here, levels), :], kinds + 2, (t, up, k))
-
-    gather(field_ref, edge_ref, gas_all, above_gas, below_gas, 2)
+    state_at = tile_ref.at[:, pl.ds(pl.multiple_of(h * own, own), own)]
+    send(state_ref, state_at, 1, (x, y, partner))
+    pltpu.make_async_copy(state_ref, state_at, recv_sem.at[1]).start()
+    gas_at = gas_ref.at[:, :, pl.ds(here, levels), :]
+    send(field_ref, gas_at, 2, (x, y, partner))
+    pltpu.make_async_copy(field_ref, gas_at, recv_sem.at[2]).start()
+
     pltpu.make_async_copy(bins_in, bins_in, recv_sem.at[0]).wait()
-    edge_rows = [[], [], [], []]
+    edge_rows = [[] for _ in range(7)]
     for i in range(rows_x):
         sums = [bins_ref[p, i, pl.ds(here, levels), :] + bins_in[p, i] for p in range(5)]
         porous = 1.0 / (1.0 + sums[0])
         inverse = 1.0 / (porous + sums[1] + 6.0 * VISCOSITY)
-        values = [porous * field_ref[c, i] + sums[2 + c] + src_ref[c, i] for c in range(3)] + [inverse]
-        for p in range(4):
-            mine[p, i] = values[p]
+        gas = [field_ref[c, i] for c in range(3)]
+        values = [porous * gas[c] + sums[2 + c] + src_ref[c, i] for c in range(3)] + [inverse] + gas
+        for p in range(7):
+            block_ref[p, i] = values[p]
             edge_rows[p].append(values[p])
-    for p in range(4):
-        mine_edge[p] = pack_edges(edge_rows[p])
-    gather(mine, mine_edge, rhs_all, above_rhs, below_rhs, 5)
-    for kind, ref in enumerate((tile_ref, gas_all, above_gas, below_gas, rhs_all, above_rhs, below_rhs)):
-        pltpu.make_async_copy(ref, ref, recv_sem.at[kind + 1]).wait()
+    for p in range(7):
+        edges[p] = pack_edges(edge_rows[p])
+    send(edges, above, 3, (x, down, h))
+    send(edges, below, 4, (x, up, h))
+    pltpu.make_async_copy(above, above, recv_sem.at[3]).wait()
+    pltpu.make_async_copy(below, below, recv_sem.at[4]).wait()
+    lane = lax.broadcasted_iota(jnp.int32, (levels, LANES), 1)
+    for p in range(7):
+        block_ref[p, rows_x] = jnp.where(lane < LANES // 2, above[p], below[p])
+    for kind, ref in ((1, tile_ref), (2, gas_ref)):
+        pltpu.make_async_copy(ref, ref, recv_sem.at[kind]).wait()
     for copy in copies:
         copy.wait_send()
 
 
+def load_table(target, load_row, rows, groups):
+    @pl.loop(0, groups // 16)
+    def _(step):
+        for r in range(rows):
+            lines = [load_row(r, step * 16 + j) for j in range(16)]
+            value = jnp.concatenate(lines, axis=0)
+            high = value.astype(jnp.bfloat16)
+            at = pl.ds(pl.multiple_of(r * groups + step * 16, 16), 16)
+            target[at, 0:LANES] = high
+            target[at, LANES : 2 * LANES] = (value - high.astype(F32)).astype(jnp.bfloat16)
+
+
+def pick(table, rows, groups, index, target):
+    n = 2
+    for q in range(SUB // n):
+        line = jnp.concatenate([index[q * n + i : q * n + i + 1] for i in range(n)], axis=1)
+        shape = (LANES, n * LANES)
+        hot = jnp.broadcast_to(line & (LANES - 1), shape) == lax.broadcasted_iota(jnp.int32, shape, 0)
+        hot = jnp.where(hot, 1.0, 0.0).astype(jnp.bfloat16)
+        hot = jnp.concatenate([hot, hot], axis=0)
+        shape = (groups, n * LANES)
+        hit = jnp.broadcast_to(line >> 7, shape) == lax.broadcasted_iota(jnp.int32, shape, 0)
+        full = jnp.dot(table[...], hot, preferred_element_type=F32)
+        for r in range(rows):
+            part = jnp.where(hit, full[r * groups : (r + 1) * groups], 0.0)
+            part = jnp.sum(part, axis=0, keepdims=True)
+            for i in range(n):
+                target[r, q * n + i : q * n + i + 1, :] = part[:, i * LANES : (i + 1) * LANES]
+
+
 def pair_kernel(
     rows_x,
-    count_ref, tile_ref, state_ref, state_rows, cell_ref, own_ref, other_ref, gas_all,
-    out_ref, force_ref,
+    count_ref, tile_ref, state_ref, state_rows, cell_ref, own_ref, other_ref, gas_ref,
+    out_ref, force_ref, own_table, tile_table, gas_table, first_ref, second_ref,
 ):
-    levels_all = gas_all.shape[2]
-    x = lax.axis_index("tx")
+    levels_all = gas_ref.shape[2]
     groups = state_ref.shape[1] // LANES
     tile_groups = tile_ref.shape[1] // LANES
+    load_table(
+        own_table, lambda r, g: state_ref[r : r + 1, pl.ds(pl.multiple_of(g * LANES, LANES), LANES)], 7, groups
+    )
+    load_table(
+        tile_table, lambda r, g: tile_ref[r : r + 1, pl.ds(pl.multiple_of(g * LANES, LANES), LANES)], 7, tile_groups
+    )
+    load_table(
+        gas_table, lambda c, g: gas_ref[c, g // levels_all, pl.ds(g % levels_all, 1), :], 3, rows_x * levels_all
+    )
     force_ref[...] = jnp.zeros_like(force_ref)
     count = count_ref[0]
-    block = PAIR_ROWS * LANES
-    chunks = PAIR_ROWS // SUB
+    block = SUB * LANES
 
     @pl.loop(0, (count + block - 1) // block)
     def _(round_index):
-        start = pl.multiple_of(round_index * PAIR_ROWS, PAIR_ROWS)
-        own = [own_ref[pl.ds(start + i * SUB, SUB), :] for i in range(chunks)]
-        other = [other_ref[pl.ds(start + i * SUB, SUB), :] for i in range(chunks)]
-        rows = range(7)
-        first = take_groups(
-            lambda r, g: state_ref[r : r + 1, pl.ds(pl.multiple_of(g * LANES, LANES), LANES)],
-            rows, groups, [v >> 7 for v in own], [v & 127 for v in own], 2,
-        )
-        second = take_groups(
-            lambda r, g: tile_ref[r : r + 1, pl.ds(pl.multiple_of(g * LANES, LANES), LANES)],
-            rows, tile_groups, [v >> 7 for v in other], [v & 127 for v in other], 2,
-        )
-        for i in range(chunks):
-            a, b = first[i], second[i]
-            gap = [a[c] - b[c] for c in range(3)]
-            distance = jnp.sqrt(gap[0] * gap[0] + gap[1] * gap[1] + gap[2] * gap[2])
-            scale = 1.0 / jnp.maximum(distance, FLOOR)
-            normal = [v * scale for v in gap]
-            overlap = jnp.maximum(a[6] + b[6] - distance, 0.0)
-            closing = sum((a[3 + c] - b[3 + c]) * normal[c] for c in range(3))
-            root = jnp.sqrt(overlap)
-            size = STIFF * overlap * root - DAMPING * root * closing
-            place = (
-                (start + i * SUB + lax.broadcasted_iota(jnp.int32, (SUB, LANES), 0)) * LANES
-                + lax.broadcasted_iota(jnp.int32, (SUB, LANES), 1)
-            )
-            size = jnp.where(place < count, size, 0.0)
-            sums = spread_dot([size * v for v in normal], own[i] >> 7, own[i] & 127, groups)
-            for c in range(3):
-                force_ref[c] += sums[c]
-
-    for i in range(groups // SUB):
-        cell = cell_ref[i * SUB : (i + 1) * SUB, :]
+        start = pl.multiple_of(round_index * SUB, SUB)
+        own = own_ref[pl.ds(start, SUB), :]
+        pick(own_table, 7, groups, own, first_ref)
+        pick(tile_table, 7, tile_groups, other_ref[pl.ds(start, SUB), :], second_ref)
+        a = [first_ref[r] for r in range(7)]
+        b = [second_ref[r] for r in range(7)]
+        gap = [a[c] - b[c] for c in range(3)]
+        distance = jnp.sqrt(gap[0] * gap[0] + gap[1] * gap[1] + gap[2] * gap[2])
+        scale = 1.0 / jnp.maximum(distance, FLOOR)
+        normal = [v * scale for v in gap]
+        overlap = jnp.maximum(a[6] + b[6] - distance, 0.0)
+        closing = sum((a[3 + c] - b[3 + c]) * normal[c] for c in range(3))
+        root = jnp.sqrt(overlap)
+        size = STIFF * overlap * root - DAMPING * root * closing
+        place = (start + lax.broadcasted_iota(jnp.int32, (SUB, LANES), 0)) * LANES
+        place = place + lax.broadcasted_iota(jnp.int32, (SUB, LANES), 1)
+        size = jnp.where(place < count, size, 0.0)
+        sums = spread_dot([size * v for v in normal], own >> 7, own & 127, groups)
+        for c in range(3):
+            force_ref[c] += sums[c]
+
+    @pl.loop(0, groups // SUB)
+    def _(i):
+        span = pl.ds(pl.multiple_of(i * SUB, SUB), SUB)
+        cell = cell_ref[span, :]
         line = cell >> 7
         high = (line % rows_x) * levels_all + line // rows_x
-        at_cell = take_groups(
-            lambda c, g: gas_all[c, x * rows_x + g // levels_all, pl.ds(g % levels_all, 1), :],
-            range(3), rows_x * levels_all, [high], [cell & 127], 4,
-        )[0]
-        span = slice(i * SUB, (i + 1) * SUB)
+        pick(gas_table, 3, rows_x * levels_all, high * LANES + (cell & 127), first_ref)
         drag = BETA_RATE * state_rows[6, span, :]
         rate = TIME_STEP / state_rows[7, span, :]
         for c in range(3):
             velocity = state_rows[3 + c, span, :]
-            value = velocity + (force_ref[c, span, :] + drag * (at_cell[c] - velocity)) * rate
+            value = velocity + (force_ref[c, span, :] + drag * (first_ref[c] - velocity)) * rate
             if c == 2:
                 value = value - TIME_STEP * GRAVITY
             out_ref[c, span, :] = value
 
 
-def sweep_kernel(
-    rows_x,
-    gas_all, rhs_all, above_gas, below_gas, above_rhs, below_rhs,
-    out_ref, field_a, field_b, rhs_ref,
-):
-    n_all, levels_all = gas_all.shape[1], gas_all.shape[2]
+def sweep_kernel(rows_x, n_h, whole, out_ref, field_a, field_b, rhs_ref):
+    n_all, levels_all = field_a.shape[1:3]
     levels = out_ref.shape[1]
     x, h = lax.axis_index("tx"), lax.axis_index("solver")
-    lane = lax.broadcasted_iota(jnp.int32, (levels_all, LANES), 1)
-
-    def fill(planes, whole, above, below, target):
-        @pl.loop(0, n_all // rows_x)
-        def _(t):
-            for p in range(planes):
-                high = above[p, t]
-                low = below[p, t]
+    lane = lax.broadcasted_iota(jnp.int32, (levels, LANES), 1)
+
+    @pl.loop(0, n_all // rows_x)
+    def _(t):
+        for k in range(n_h):
+            span = slice(k * levels, (k + 1) * levels)
+            for p in range(7):
+                target, q = (rhs_ref, p) if p < 4 else (field_a, p - 4)
+                edge_row = whole[t * n_h + k, p, rows_x]
                 for i in range(rows_x):
                     at = t * rows_x + i
-                    target[p, at, :, 0:LANES] = whole[p, at]
-                    right = pltpu.roll(high, (LANES - i * HALO) % LANES, axis=1)
-                    left = pltpu.roll(low, (LANES // 2 - (i + 1) * HALO) % LANES, axis=1)
+                    target[q, at, span, 0:LANES] = whole[t * n_h + k, p, i]
+                    right = pltpu.roll(edge_row, (LANES - i * HALO) % LANES, axis=1)
+                    left = pltpu.roll(edge_row, (LANES // 2 - (i + 1) * HALO) % LANES, axis=1)
                     edge = jnp.where(lane < HALO, right, jnp.where(lane >= LANES - HALO, left, 0.0))
-                    target[p, at, :, LANES : 2 * LANES] = edge
-
-    fill(3, gas_all, above_gas, below_gas, field_a)
-    fill(4, rhs_all, above_rhs, below_rhs, rhs_ref)
+                    target[q, at, span, LANES : 2 * LANES] = edge
+
     level = lax.broadcasted_iota(jnp.int32, (levels_all, 2 * LANES), 0)
 
     def sweep(source, target):
@@ -389,14 +394,14 @@
     smem = pl.BlockSpec(memory_space=pltpu.SMEM)
     params = functools.partial(pltpu.CompilerParams, vmem_limit_bytes=VMEM_LIMIT)
     cells = particle_cell.reshape(-1, LANES)
-    ghosts, bins, field, source, edges = pl.pallas_call(
+    ghosts, bins, field, source = pl.pallas_call(
         functools.partial(local_kernel, levels_all, rows_x),
         out_shape=(
             shape(8, cycle), shape(5, rows_x, levels_all, rows_y), shape(3, rows_x, levels, rows_y),
-            shape(3, rows_x, levels, rows_y), shape(3, levels, LANES),
+            shape(3, rows_x, levels, rows_y),
         ),
         in_specs=[smem] + vmem_specs(5),
-        out_specs=tuple(vmem_specs(5)),
+        out_specs=tuple(vmem_specs(4)),
         compiler_params=params(),
         name="local",
     )(
@@ -404,44 +409,52 @@
         gas_velocity, gas_source,
     )
     n_all = n_x * rows_x
-    ring = n_x * n_h
-    sends = 2 + 10 * n_h + 2 * (ring - 1 + 2 * ring)
-    tile, gas_all, rhs_all, above_gas, below_gas, above_rhs, below_rhs = pl.pallas_call(
+    sends = 5 + 10 * n_h
+    tile, gas_own, block = pl.pallas_call(
         functools.partial(exchange_kernel, sizes),
         out_shape=(
-            shape(8, n_h * (own + cycle)),
-            shape(3, n_all, levels_all, rows_y), shape(4, n_all, levels_all, rows_y),
-            shape(3, n_x, levels_all, LANES), shape(3, n_x, levels_all, LANES),
-            shape(4, n_x, levels_all, LANES), shape(4, n_x, levels_all, LANES),
+            shape(8, n_h * (own + cycle)), shape(3, rows_x, levels_all, rows_y),
+            shape(7, rows_x + 1, levels, rows_y),
         ),
-        in_specs=vmem_specs(6),
-        out_specs=tuple(vmem_specs(7)),
+        in_specs=vmem_specs(5),
+        out_specs=tuple(vmem_specs(3)),
         scratch_shapes=[
             pltpu.VMEM((5, rows_x, levels, rows_y), F32),
-            pltpu.VMEM((4, rows_x, levels, rows_y), F32),
-            pltpu.VMEM((4, levels, LANES), F32),
+            pltpu.VMEM((7, levels, LANES), F32),
+            pltpu.VMEM((7, levels, LANES), F32),
+            pltpu.VMEM((7, levels, LANES), F32),
             pltpu.SemaphoreType.DMA((sends,)),
-            pltpu.SemaphoreType.DMA((8,)),
+            pltpu.SemaphoreType.DMA((5,)),
         ],
         compiler_params=params(collective_id=0, has_side_effects=True),
         name="exchange",
-    )(particle_state, ghosts, bins, field, source, edges)
+    )(particle_state, ghosts, bins, field, source)
+    whole = lax.all_gather(block, ("tx", "solver"))
+    tile_groups = tile.shape[1] // LANES
     moved = pl.pallas_call(
         functools.partial(pair_kernel, rows_x),
         out_shape=shape(3, own // LANES, LANES),
         in_specs=[smem] + vmem_specs(7),
         out_specs=vmem_specs(1)[0],
-        scratch_shapes=[pltpu.VMEM((3, own // LANES, LANES), F32)],
+        scratch_shapes=[
+            pltpu.VMEM((3, own // LANES, LANES), F32),
+            pltpu.VMEM((7 * own // LANES, 2 * LANES), jnp.bfloat16),
+            pltpu.VMEM((7 * tile_groups, 2 * LANES), jnp.bfloat16),
+            pltpu.VMEM((3 * rows_x * levels_all, 2 * LANES), jnp.bfloat16),
+            pltpu.VMEM((7, SUB, LANES), F32),
+            pltpu.VMEM((7, SUB, LANES), F32),
+        ],
         compiler_params=params(),
+        cost_estimate=pl.CostEstimate(flops=10**10, bytes_accessed=10**8, transcendentals=0),
         name="pairs",
     )(
         contact_count.reshape(1), tile, particle_state, particle_state.reshape(8, -1, LANES), cells,
-        contact_own.reshape(-1, LANES), contact_other.reshape(-1, LANES), gas_all,
+        contact_own.reshape(-1, LANES), contact_other.reshape(-1, LANES), gas_own,
     )
     swept = pl.pallas_call(
-        functools.partial(sweep_kernel, rows_x),
+        functools.partial(sweep_kernel, rows_x, n_h),
         out_shape=shape(3, levels, rows_x, rows_y),
-        in_specs=vmem_specs(6),
+        in_specs=vmem_specs(1),
         out_specs=vmem_specs(1)[0],
         scratch_shapes=[
             pltpu.VMEM((3, n_all, levels_all, 2 * LANES), F32),
@@ -450,7 +463,7 @@
         ],
         compiler_params=params(),
         name="sweeps",
-    )(gas_all, rhs_all, above_gas, below_gas, above_rhs, below_rhs)
+    )(whole)
     return (moved.reshape(3, own), swept)
 
 

time: 108 us -> 80.7 us (0.75)
  the two profiles are of different devices: /device:TPU:4 before, /device:TPU:0 now
where the time goes in v2:
time: 80.7 us; the launch traced here: 80.2 us
  Pallas kernels  40.7 us (50%)
  waiting for transfers between devices  15.4 us (19%)
  between operations  14.7 us (18%)
  local copies, waits for them, and re-layouts  9.27 us (11%)
    pallas_call x1, Pallas kernels, on_device(): pl.pallas_call(functools.partial(sweep_kernel, rows_x, n_h), out_shape=sh...  16.9 us
    pallas_call x1, Pallas kernels, on_device(): pl.pallas_call(functools.partial(exchange_kernel, sizes), out_shape=(shap...  16.7 us
    all_gather x1, waiting for transfers between devices, on_device(): whole = lax.all_gather(block, ('tx', 'solver'))  15.4 us
    unnamed x22, local copies, waits for them, and re-layouts  7.82 us
    pallas_call x1, Pallas kernels, on_device(): pl.pallas_call(functools.partial(pair_kernel, rows_x), out_shape=shape(3,...  4.23 us
    pallas_call x1, Pallas kernels, on_device(): pl.pallas_call(functools.partial(local_kernel, levels_all, rows_x), out_s...  2.94 us
  transfers between devices with their start and end apart: 1, of which 1 were waited for; matrix products, arithmetic and copies ran while one was open for 2% of the time, Pallas kernels for 5%

profile of v2, /device:TPU:0, one launch (start us, length us, event | category | flops | bytes accessed | tf_op | source)
XLA Modules:
  0.0 80.2 jit_solution(12256794915939701460)
XLA Ops:
  7.2 0.0 all-gather.3.cloned.1.call-start
  7.2 0.8 reshape.29.count_ref
  8.0 0.7 reshape.31.list_ref
  8.7 0.9 %copy-done = f32[8,4096]{1,0:T(8,128)S(1)} copy-done((f32[8,4096]{1,0:T(8,128)S(1)}, f32[8,4096]{1,0:T(8,128)}, u32[]{:S(2)}) %copy-start) | copy-done | bytes 131096
  9.6 0.0 copy-start.4
  9.6 0.8 copy-done.4
  10.4 0.8 copy-done.5
  11.2 0.7 copy-done.6
  11.9 2.9 %local.1 = (f32[8,3072]{1,0:T(8,128)S(1)}, f32[5,4,16,128]{3,2,1,0:T(8,128)S(1)}, f32[3,4,8,128]{3,2,1,0:T(8,128)S(1)}, f32[3,4,8,128]{3,2,1,0:T(8,128)S(1)}) custom-call(s32[4]{0:T(128)S(1)} %reshape.29.count_ref, f32[8,4096]{1,0:T(8,128)S(1)} %copy-done, s32[32,128]{1,0:T(8,128)S(1)} %bitcast.18, s32[8,128]{1,0:T(8,128)S(1)} %reshape.31.list_ref, ...), custom_call_target="tpu_custom_call" | custom-call | tf_op jit(solution)/shard_map/local/pallas_call | solution.py:397
  14.8 0.0 copy-start.1
  14.8 0.9 %copy-done.1 = f32[8,4096]{1,0:T(8,128)S(1)} copy-done((f32[8,4096]{1,0:T(8,128)S(1)}, f32[8,4096]{1,0:T(8,128)}, u32[]{:S(2)}) %copy-start.1) | copy-done | bytes 131096
  15.7 16.7 %exchange.1 = (f32[8,14336]{1,0:T(8,128)S(1)}, f32[3,4,16,128]{3,2,1,0:T(8,128)S(1)}, f32[7,5,8,128]{3,2,1,0:T(8,128)}) custom-call(f32[8,4096]{1,0:T(8,128)S(1)} %copy-done.1, f32[8,3072]{1,0:T(8,128)S(1)} %get-tuple-element.9.ghost_ref, f32[5,4,16,128]{3,2,1,0:T(8,128)S(1)} %get-tuple-element.10.bins_ref, ...), custom_call_target="tpu_custom_call" | custom-call | tf_op jit(solution)/shard_map/exchange/pallas_call | solution.py:413
  32.4 0.0 all-gather.3.cloned.1.call-update
  33.1 0.9 %copy.15 = f32[1,8,32,128]{3,2,1,0:T(8,128)S(1)} copy(f32[1,8,32,128]{3,1,2,0:T(8,128)} %bitcast.14) | data formatting | bytes 262144
  34.0 0.0 copy-done.2
  34.1 0.0 copy-done.7
  34.1 0.0 copy-done.8
  34.1 0.0 copy-start.9
  34.1 0.8 %copy-done.9 = s32[1,1,1,16384]{3,2,1,0:T(1,128)S(1)} copy-done((s32[1,1,1,16384]{3,2,1,0:T(1,128)S(1)}, s32[1,1,1,16384]{3,2,1,0:T(1,128)}, u32[]{:S(2)}) %copy-start.9) | copy-done | bytes 65560
  34.9 4.2 %pairs.1 = f32[3,32,128]{2,1,0:T(8,128)S(1)} custom-call(s32[1]{0:T(128)} %bitcast.13.count_ref, f32[8,14336]{1,0:T(8,128)S(1)} %get-tuple-element.13.tile_ref, f32[8,4096]{1,0:T(8,128)S(1)} %copy-done.2, f32[8,32,128]{2,1,0:T(8,128)S(1)} %bitcast.16, s32[32,128]{1,0:T(8,128)S(1)} %bitcast.19, s32[128,128]{1,0:T(8,128)S(1)} %bitcast.20, ...), custom_call_target="tpu_custom_call" | custom-call | flops 10000000000 | bytes 100000000 | tf_op jit(solution)/shard_map/pairs/pallas_call | solution.py:434
  39.2 0.7 copy.16
  39.8 15.4 %all-gather.3.cloned.1.call-done = f32[56,5,8,128]{3,2,1,0:T(8,128)} async-done(((f32[7,5,8,128]{3,2,1,0:T(8,128)}), f32[56,5,8,128]{3,2,1,0:T(8,128)}) %all-gather.3.cloned.1.call-update) | async-done | bytes 1146896 | tf_op jit(solution)/shard_map/all_gather | solution.py:432
  55.2 1.3 %copy-done.3 = f32[56,5,8,128]{3,2,1,0:T(8,128)S(1)} copy-done((f32[56,5,8,128]{3,2,1,0:T(8,128)S(1)}, f32[56,5,8,128]{3,2,1,0:T(8,128)}, u32[]{:S(2)}) %copy-start.3) | copy-done | bytes 1146904
  56.5 16.9 %sweeps.1 = f32[3,8,4,128]{3,2,1,0:T(4,128)} custom-call(f32[8,7,5,8,128]{4,3,2,1,0:T(8,128)S(1)} %bitcast.15), custom_call_target="tpu_custom_call" | custom-call | tf_op jit(solution)/shard_map/sweeps/pallas_call | solution.py:454
  (7 shorter events, 0.0 us)
Async XLA Ops:
  7.2 48.0 %all-gather.3.cloned.1.call-start = ((), (), s32[]{:S(2)}) async-start(), calls=%async_computation | async-start | bytes 1290240 | tf_op jit(solution)/shard_map/all_gather | solution.py:432
  8.7 0.9 %copy-start = (f32[8,4096]{1,0:T(8,128)S(1)}, f32[8,4096]{1,0:T(8,128)}, u32[]{:S(2)}) copy-start(f32[8,4096]{1,0:T(8,128)} %state_ref.5) | copy-start | bytes 393220
  9.6 0.8 copy-start.4
  10.4 0.8 copy-start.5
  11.2 0.7 copy-start.6
  11.9 22.2 %copy-start.2 = (f32[8,4096]{1,0:T(8,128)S(1)}, f32[8,4096]{1,0:T(8,128)}, u32[]{:S(2)}) copy-start(f32[8,4096]{1,0:T(8,128)} %state_ref.5) | copy-start | bytes 393220
  11.9 22.2 %copy-start.7 = (s32[4096]{0:T(1024)S(1)}, s32[4096]{0:T(1024)}, u32[]{:S(2)}) copy-start(s32[4096]{0:T(1024)} %param.10) | copy-start | bytes 49156
  11.9 22.2 %copy-start.8 = (s32[1,1,1,16384]{3,2,1,0:T(1,128)S(1)}, s32[1,1,1,16384]{3,2,1,0:T(1,128)}, u32[]{:S(2)}) copy-start(s32[1,1,1,16384]{3,2,1,0:T(1,128)} %param.13) | copy-start | bytes 196612
  14.8 0.9 %copy-start.1 = (f32[8,4096]{1,0:T(8,128)S(1)}, f32[8,4096]{1,0:T(8,128)}, u32[]{:S(2)}) copy-start(f32[8,4096]{1,0:T(8,128)} %state_ref.5) | copy-start | bytes 393220
  34.1 0.8 %copy-start.9 = (s32[1,1,1,16384]{3,2,1,0:T(1,128)S(1)}, s32[1,1,1,16384]{3,2,1,0:T(1,128)}, u32[]{:S(2)}) copy-start(s32[1,1,1,16384]{3,2,1,0:T(1,128)} %param.14) | copy-start | bytes 196612
  55.2 1.3 %copy-start.3 = (f32[56,5,8,128]{3,2,1,0:T(8,128)S(1)}, f32[56,5,8,128]{3,2,1,0:T(8,128)}, u32[]{:S(2)}) copy-start(f32[56,5,8,128]{3,2,1,0:T(8,128)} %all-gather.3.cloned.1.call-done) | copy-start | bytes 3440644
Sparse Core Ops, SparseCore 0:
  32.6 22.5 all-gather.2
